TPU v7x, 256 devices: a whole 4x4x8 slice. The times are simulated.
256 devices in a mesh: rows: 64 (over x, z, core), cols: 4 (over y).
Axes of the slice: x: 4, y: 4, z: 8, core: 2. Of those that a mesh axis runs over, the one named last changes fastest.
Arguments:
- column_lists: int32 [256, 13], replicated, may hold values from -1 to 255, as said below
- block_values: bfloat16 [256, 13, 128, 128], P('rows'), as said below
Outputs:
- purified: bfloat16 [256, 13, 128, 128], P('rows', None, None, 'cols')
Inputs may be any that keep to these rules, and one draw needn't show every extreme that they name: `column_lists`: slot (13 - 1) // 2 of row i holds i. Slot s of row i holds -1 or a row j, and then slot 12 - s of row j holds i. There is an ordering of the rows, taken cyclically, in which the row in slot s of row i stands s - (13 - 1) // 2 places after row i. With owners the aligned groups of 4 rows, the slots of one owner's rows hold at most 2 rows of any one other owner, and some pair of owners has exactly 2. Over the slots s of one owner's rows that hold rows of one other owner, the sum of 13 - |s - (13 - 1) // 2| is at most 16, and exactly 16 for some pair of owners. block_values[j, 12 - s] is the transpose of block_values[i, s] where slot s of row i holds j; blocks of empty slots are zero.
All inputs are finite; a program needn't handle non-finite values.
Results may differ from a plain program's by a relative error of at most 0.0039.
Values may be sent and summed in bfloat16 or wider, within the bound.
No kernel may reach another device: no remote copies, remote signals or barrier semaphores. Data moves between devices by JAX's collectives and lax.ppermute only.
A program may use at most 128 MiB of HBM per device.

v0:
```python
import jax
import jax.numpy as jnp
from jax import lax
from jax.sharding import PartitionSpec as P

CAP = 2


def body(column_lists, block_values):
    rows_here = block_values.shape[0]
    slot_count = block_values.shape[1]
    block_size = block_values.shape[2]
    middle = (slot_count - 1) // 2
    owners = lax.axis_size("rows")
    strip_width = block_size // lax.axis_size("cols")
    row_index = lax.axis_index("rows")
    column_part = lax.axis_index("cols")
    all_rows = column_lists.shape[0]
    present = column_lists >= 0
    target = jnp.maximum(column_lists, 0)
    owner_of = target // rows_here
    home_owner = (jnp.arange(all_rows, dtype=jnp.int32) // rows_here)[:, None]
    crossing = present & (owner_of != home_owner)
    dest_hot = (
        crossing[:, :, None] & (owner_of[:, :, None] == jnp.arange(owners, dtype=jnp.int32))
    ).astype(jnp.int32)
    first_row = row_index * rows_here
    own_present = lax.dynamic_slice_in_dim(present, first_row, rows_here, 0)
    my_cross = lax.dynamic_slice_in_dim(crossing, first_row, rows_here, 0)
    my_owner = lax.dynamic_slice_in_dim(owner_of, first_row, rows_here, 0)
    my_target = lax.dynamic_slice_in_dim(target, first_row, rows_here, 0)
    full_rows = jnp.where(
        own_present[:, :, None, None], block_values, jnp.zeros((), block_values.dtype)
    )
    own_strip = lax.dynamic_slice_in_dim(full_rows, column_part * strip_width, strip_width, 3)
    slot_ids = jnp.arange(slot_count, dtype=jnp.int32)
    running = jnp.cumsum(dest_hot.reshape(owners, rows_here * slot_count, owners), axis=1)
    running = running.reshape(all_rows, slot_count, owners)
    ranking = jnp.sum(running * dest_hot, axis=2) - 1
    my_rank = lax.dynamic_slice_in_dim(ranking, first_row, rows_here, 0)
    filler = jnp.zeros((1, slot_count - 1, block_size, strip_width), own_strip.dtype)
    local_stack = jnp.concatenate([own_strip[:, : slot_count - 1], own_strip[:, 1:], filler], 0)
    zero_entry = 2 * rows_here
    slot_of = jnp.where(my_cross, my_owner * CAP + my_rank, owners * CAP)
    stack_entry = (
        jnp.arange(rows_here, dtype=jnp.int32)[:, None]
        + jnp.where(slot_ids < middle, 0, rows_here)[None, :]
    )
    source = jnp.full((owners * CAP + 1,), zero_entry, jnp.int32)
    source = source.at[slot_of.reshape(-1)].set(stack_entry.reshape(-1))[: owners * CAP]
    outgoing = local_stack[source]
    back_rank = ranking[my_target, (slot_count - 1 - slot_ids)[None, :]]
    local_pick = (
        owners * CAP + my_target - first_row + jnp.where(slot_ids > middle, 0, rows_here)[None, :]
    )
    remote_pick = my_owner * CAP + back_rank
    empty_entry = owners * CAP + zero_entry
    table_pick = jnp.where(
        own_present & (my_owner == row_index),
        local_pick,
        jnp.where(own_present, remote_pick, empty_entry),
    )
    table_pick = table_pick.at[:, middle].set(empty_entry)
    arrived = lax.all_to_all(outgoing, "rows", split_axis=0, concat_axis=0, tiled=True)
    lookup = jnp.concatenate([arrived, local_stack], 0)
    picked = lookup[table_pick]
    by_slot = []
    for slot_index in range(slot_count):
        offset = slot_index - middle
        if offset == 0:
            by_slot.append(own_strip)
        elif offset > 0:
            by_slot.append(
                jnp.pad(
                    picked[:, slot_index, : slot_count - offset],
                    ((0, 0), (offset, 0), (0, 0), (0, 0)),
                )
            )
        else:
            by_slot.append(
                jnp.pad(
                    picked[:, slot_index, -offset - 1 :], ((0, 0), (0, -offset), (0, 0), (0, 0))
                )
            )
    windows = jnp.stack(by_slot, 1)
    square_sum = jnp.einsum(
        "iapq,iasqc->ispc", full_rows, windows, preferred_element_type=jnp.float32
    )
    square = jnp.where(own_present[:, :, None, None], square_sum, 0.0).astype(jnp.bfloat16)
    cube_sum = jnp.einsum(
        "iapq,iasqc->ispc",
        lax.all_gather(square, "cols", axis=3, tiled=True),
        windows,
        preferred_element_type=jnp.float32,
    )
    purified = jnp.where(
        own_present[:, :, None, None], 3.0 * square.astype(jnp.float32) - 2.0 * cube_sum, 0.0
    )
    return purified.astype(jnp.bfloat16)


def solution(mesh):
    in_specs = (P(), P("rows", None, None, None))
    out_specs = P("rows", None, None, "cols")
    return jax.shard_map(body, mesh=mesh, in_specs=in_specs, out_specs=out_specs, check_vma=False)
```

profile of v0, /device:TPU:1, one launch (start us, length us, event | category | flops | bytes accessed | tf_op | source)
XLA Modules:
  0.0 390.3 jit_solution(5772552660954711740)
XLA Ops:
  6.6 0.8 copy.54
  8.1 2.7 select_reduce_fusion
  11.0 1.0 gather_fusion.1
  12.1 2.8 copy.55
  15.1 0.7 scatter_custom_fusion
  16.2 1.1 copy-done
  17.6 8.0 %gather_fusion = bf16[128,12,128,32]{2,3,1,0:T(8,128)(2,1)} fusion(bf16[9,12,128,32]{2,3,1,0:T(8,128)(2,1)S(1)} %pad_maximum_fusion.1, s32[1024]{0:T(1024)S(1)} %pad_clamp_fusion.1), kind=kCustom, calls=%fused_computation | custom fusion | bytes 25166336 | tf_op jit(solution)/shard_map/gather | solution.py:51
  25.7 13.3 %all-to-all-start = ((bf16[128,12,128,32]{2,3,1,0:T(8,128)(2,1)}), bf16[128,12,128,32]{2,3,1,0:T(8,128)(2,1)}, u32[]{:S(2)}, u32[]{:S(2)}) async-start(bf16[128,12,128,32]{2,3,1,0:T(8,128)(2,1)} %gather_fusion), calls=%async_computation | async-start | bytes 25165824 | tf_op jit(solution)/shard_map/all_to_all | solution.py:64
  39.0 0.7 compare_reduce_fusion
  39.7 0.8 slice_select_fusion
  40.8 273.8 %all-to-all-done = bf16[128,12,128,32]{2,3,1,0:T(8,128)(2,1)} async-done(((bf16[128,12,128,32]{2,3,1,0:T(8,128)(2,1)}), bf16[128,12,128,32]{2,3,1,0:T(8,128)(2,1)}, u32[]{:S(2)}, u32[]{:S(2)}) %all-to-all-start) | async-done | bytes 12582944 | tf_op jit(solution)/shard_map/all_to_all | solution.py:64
  314.6 14.4 %pad_maximum_fusion = bf16[137,12,128,32]{2,3,1,0:T(8,128)(2,1)} fusion(bf16[1,12,128,32]{2,3,1,0:T(8,128)(2,1)S(1)} %broadcast_in_dim.85, bf16[4,12,128,32]{2,3,1,0:T(8,128)(2,1)S(1)} %copy-done.4, bf16[4,12,128,32]{2,3,1,0:T(8,128)(2,1)S(1)} %copy-done.2, bf16[128,12,128,32]{2,3,1,0:T(8,128)(2,1)} %all-to-all-done), kind=kLoop, calls=%fused_computation.4 | loop fusion | flops 20201472 | bytes 26935296 | tf_op jit(solution)/shard_map/concatenate | solution.py:65
  329.0 8.4 %gather_fusion.2 = bf16[52,12,128,32]{2,3,1,0:T(8,128)(2,1)} fusion(bf16[137,12,128,32]{2,3,1,0:T(8,128)(2,1)} %pad_maximum_fusion, s32[1024]{0:T(1024)S(1)} %pad_clamp_fusion), kind=kCustom, calls=%fused_computation.2 | custom fusion | bytes 10223824 | tf_op jit(solution)/shard_map/gather | solution.py:66
  337.4 1.1 slice_bitcast_fusion.10
  338.4 1.1 slice_bitcast_fusion.8
  339.5 1.1 slice_bitcast_fusion.6
  340.6 1.1 slice_bitcast_fusion.4
  341.7 1.1 slice_bitcast_fusion.2
  342.9 1.2 slice_bitcast_fusion
  344.5 1.1 bitcast_dynamic-update-slice_fusion.6
  346.1 2.4 copy-done.5
  348.5 2.4 fusion.35
  350.9 27.1 %all-gather.2.cloned.1.call-done = bf16[4,13,128,128]{2,3,1,0:T(8,128)(2,1)} async-done(((bf16[4,13,128,32]{2,3,1,0:T(8,128)(2,1)}), bf16[4,13,128,128]{2,3,1,0:T(8,128)(2,1)}) %all-gather.2.cloned.1.call-update) | async-done | bytes 1703952 | tf_op jit(solution)/shard_map/all_gather | solution.py:92
  378.0 5.4 %fusion.26 = bf16[4,13,128,32]{2,3,1,0:T(8,128)(2,1)} fusion(bf16[4,13,13,128,32]{3,4,1,2,0:T(8,128)(2,1)} %copy-done.5, bf16[4,13,128,128]{2,3,1,0:T(8,128)(2,1)} %all-gather.2.cloned.1.call-done, bf16[4,13,128,32]{2,3,1,0:T(8,128)(2,1)} %fusion.35, pred[4,13]{1,0:T(4,128)(4,1)S(1)} %get-tuple-element.18), kind=kOutput, calls=%fused_computation.21 | convolution fusion | flops 710115328 | bytes 8093748 | tf_op jit(solution)/shard_map/iapq,iasqc->ispc/dot_general | solution.py:90
  (54 shorter events, 3.0 us)
Async XLA Ops:
  16.1 1.2 copy-start
  16.2 1.2 copy-start.1
  16.2 1.3 copy-start.3
  25.7 288.9 %copy-start.2 = (bf16[4,12,128,32]{2,3,1,0:T(8,128)(2,1)S(1)}, bf16[4,12,128,32]{2,3,1,0:T(8,128)(2,1)}, u32[]{:S(2)}) copy-start(bf16[4,12,128,32]{2,3,1,0:T(8,128)(2,1)} %copy-done.1) | copy-start | bytes 1179652
  25.7 288.9 %copy-start.4 = (bf16[4,12,128,32]{2,3,1,0:T(8,128)(2,1)S(1)}, bf16[4,12,128,32]{2,3,1,0:T(8,128)(2,1)}, u32[]{:S(2)}) copy-start(bf16[4,12,128,32]{2,3,1,0:T(8,128)(2,1)} %copy-done.3) | copy-start | bytes 1179652
  25.7 288.9 %all-to-all-start = ((bf16[128,12,128,32]{2,3,1,0:T(8,128)(2,1)}), bf16[128,12,128,32]{2,3,1,0:T(8,128)(2,1)}, u32[]{:S(2)}, u32[]{:S(2)}) async-start(bf16[128,12,128,32]{2,3,1,0:T(8,128)(2,1)} %gather_fusion), calls=%async_computation | async-start | bytes 25165824 | tf_op jit(solution)/shard_map/all_to_all | solution.py:64
  38.9 339.1 %all-gather.2.cloned.1.call-start = ((), (), s32[]{:S(2)}) async-start(), calls=%async_computation.1 | async-start | bytes 2129920 | tf_op jit(solution)/shard_map/all_gather | solution.py:92
  346.1 2.4 copy-start.5
Sparse Core Ops, SparseCore 0:
  351.0 26.9 all-gather.1
where the time goes:
time: 391 us; the launch traced here: 390 us
  waiting for transfers between devices  301 us (77%)
  local copies, waits for them, and re-layouts  35.4 us (9%)
  other arithmetic  19.1 us (5%)
  between operations  13.7 us (4%)
  starting transfers between devices  13.3 us (3%)
  matrix products  7.86 us (2%)
    all_to_all x1, waiting for transfers between devices, body(): lax.all_to_all(outgoing, 'rows', split_axis=0, concat_axis=0, tiled=True)  274 us
    all_gather x1, waiting for transfers between devices, body(): lax.all_gather(square, 'cols', axis=3, tiled=True)  27.1 us
    concatenate x1, other arithmetic, body(): lookup = jnp.concatenate([arrived, local_stack], 0)  14.4 us
    all_to_all x1, starting transfers between devices, body(): lax.all_to_all(outgoing, 'rows', split_axis=0, concat_axis=0, tiled=True)  13.3 us
    unnamed x26, local copies, waits for them, and re-layouts  9.2 us
    gather x1, local copies, waits for them, and re-layouts, body(): picked = lookup[table_pick]  8.37 us
    gather x1, local copies, waits for them, and re-layouts, body(): outgoing = local_stack[source]  8.05 us
  transfers between devices with their start and end apart: 2, of which 2 were waited for; matrix products, arithmetic and copies ran while one was open for 0% of the time, Pallas kernels for 0%

commit v1 on v0

--- a/solution.py
+++ b/solution.py
@@ -89,7 +89,9 @@
     square = jnp.where(own_present[:, :, None, None], square_sum, 0.0).astype(jnp.bfloat16)
     cube_sum = jnp.einsum(
         "iapq,iasqc->ispc",
-        lax.all_gather(square, "cols", axis=3, tiled=True),
+        jnp.concatenate(
+            lax.all_to_all(jnp.stack([square] * lax.axis_size("cols")), "cols", 0, 0), axis=3
+        ),
         windows,
         preferred_element_type=jnp.float32,
     )

time: 391 us -> 371 us (0.949)
  waiting for transfers between devices: 301 us -> 274 us
  blocking collectives: 0 us -> 26.4 us
  between operations: 13.7 us -> 0.34 us
    all_gather x1 -> x0, waiting for transfers between devices: 27.1 us -> none  [body(): lax.all_gather(square, 'cols', axis=3, tiled=True)]
    all_to_all x0 -> x1, blocking collectives: none -> 26.4 us  [body(): lax.all_to_all(jnp.stack([square] * lax.axis_size('cols')), 'cols', 0, 0)]
    unnamed x26 -> x24, local copies, waits for them, and re-layouts: 9.2 us -> 6.78 us
  transfers between devices with their start and end apart: 2 -> 1, of which waited for: 2 -> 1; matrix products, arithmetic and copies ran while one was open for 0% -> 0% of each run, Pallas kernels for 0% -> 0%
where the time goes in v1:
time: 371 us
  waiting for transfers between devices  274 us (74%)
  local copies, waits for them, and re-layouts  33.8 us (9%)
  blocking collectives  26.4 us (7%)
  other arithmetic  19 us (5%)
  starting transfers between devices  13.3 us (4%)
  matrix products  4.02 us (1%)
    all_to_all x1, waiting for transfers between devices, body(): lax.all_to_all(outgoing, 'rows', split_axis=0, concat_axis=0, tiled=True)  274 us
    all_to_all x1, blocking collectives, body(): lax.all_to_all(jnp.stack([square] * lax.axis_size('cols')), 'cols', 0, 0)  26.4 us
    concatenate x1, other arithmetic, body(): lookup = jnp.concatenate([arrived, local_stack], 0)  14.4 us
    all_to_all x1, starting transfers between devices, body(): lax.all_to_all(outgoing, 'rows', split_axis=0, concat_axis=0, tiled=True)  13.3 us
    gather x1, local copies, waits for them, and re-layouts, body(): picked = lookup[table_pick]  8.38 us
    gather x1, local copies, waits for them, and re-layouts, body(): outgoing = local_stack[source]  8.05 us
  transfers between devices with their start and end apart: 1, of which 1 were waited for; matrix products, arithmetic and copies ran while one was open for 0% of the time, Pallas kernels for 0%

profile of v1, /device:TPU:1, one launch (start us, length us, event | category | flops | bytes accessed | tf_op | source)
XLA Modules:
  0.0 370.8 jit_solution(6866481022524670520)
XLA Ops:
  0.0 0.8 copy.57
  1.6 2.7 select_reduce_fusion
  4.5 1.0 gather_fusion.1
  5.5 2.8 copy.58
  8.6 0.7 scatter_custom_fusion
  9.7 1.1 copy-done
  11.1 8.0 %gather_fusion = bf16[128,12,128,32]{2,3,1,0:T(8,128)(2,1)} fusion(bf16[9,12,128,32]{2,3,1,0:T(8,128)(2,1)S(1)} %pad_maximum_fusion.1, s32[1024]{0:T(1024)S(1)} %pad_clamp_fusion.1), kind=kCustom, calls=%fused_computation | custom fusion | bytes 25166336 | tf_op jit(solution)/shard_map/gather | solution.py:51
  19.1 13.3 %all-to-all-start = ((bf16[128,12,128,32]{2,3,1,0:T(8,128)(2,1)}), bf16[128,12,128,32]{2,3,1,0:T(8,128)(2,1)}, u32[]{:S(2)}, u32[]{:S(2)}) async-start(bf16[128,12,128,32]{2,3,1,0:T(8,128)(2,1)} %gather_fusion), calls=%async_computation | async-start | bytes 25165824 | tf_op jit(solution)/shard_map/all_to_all | solution.py:64
  32.4 0.7 compare_reduce_fusion
  33.1 0.7 slice_select_fusion
  34.1 274.0 %all-to-all-done = bf16[128,12,128,32]{2,3,1,0:T(8,128)(2,1)} async-done(((bf16[128,12,128,32]{2,3,1,0:T(8,128)(2,1)}), bf16[128,12,128,32]{2,3,1,0:T(8,128)(2,1)}, u32[]{:S(2)}, u32[]{:S(2)}) %all-to-all-start) | async-done | bytes 12582944 | tf_op jit(solution)/shard_map/all_to_all | solution.py:64
  308.1 14.4 %pad_maximum_fusion = bf16[137,12,128,32]{2,3,1,0:T(8,128)(2,1)} fusion(bf16[1,12,128,32]{2,3,1,0:T(8,128)(2,1)S(1)} %broadcast_in_dim.85, bf16[4,12,128,32]{2,3,1,0:T(8,128)(2,1)S(1)} %copy-done.4, bf16[4,12,128,32]{2,3,1,0:T(8,128)(2,1)S(1)} %copy-done.2, bf16[128,12,128,32]{2,3,1,0:T(8,128)(2,1)} %all-to-all-done), kind=kLoop, calls=%fused_computation.4 | loop fusion | flops 20201472 | bytes 26935296 | tf_op jit(solution)/shard_map/concatenate | solution.py:65
  322.5 8.4 %gather_fusion.2 = bf16[52,12,128,32]{2,3,1,0:T(8,128)(2,1)} fusion(bf16[137,12,128,32]{2,3,1,0:T(8,128)(2,1)} %pad_maximum_fusion, s32[1024]{0:T(1024)S(1)} %pad_clamp_fusion), kind=kCustom, calls=%fused_computation.2 | custom fusion | bytes 10223824 | tf_op jit(solution)/shard_map/gather | solution.py:66
  330.9 1.1 slice_bitcast_fusion.10
  331.9 1.1 slice_bitcast_fusion.8
  333.0 1.1 slice_bitcast_fusion.6
  334.1 1.1 slice_bitcast_fusion.4
  335.2 1.1 slice_bitcast_fusion.2
  336.4 1.2 slice_bitcast_fusion
  338.0 1.1 bitcast_dynamic-update-slice_fusion.6
  339.6 1.7 fusion.20
  341.5 26.4 %all_to_all.10 = bf16[4,4,13,128,32]{3,4,2,1,0:T(8,128)(2,1)S(1)} all-to-all(bf16[4,4,13,128,32]{3,4,2,1,0:T(8,128)(2,1)S(1)} %stack.63), channel_id=1, replica_groups=mesh['rows'=64,'cols'=4] {'cols'}, dimensions={0} | all-to-all | bytes 3407872 | tf_op jit(solution)/shard_map/all_to_all | solution.py:93
  367.9 0.5 copy.76
  368.4 2.4 fusion.13
  (52 shorter events, 3.2 us)
Async XLA Ops:
  9.5 1.2 copy-start
  9.6 1.2 copy-start.1
  9.7 1.3 copy-start.3
  19.1 288.9 %copy-start.2 = (bf16[4,12,128,32]{2,3,1,0:T(8,128)(2,1)S(1)}, bf16[4,12,128,32]{2,3,1,0:T(8,128)(2,1)}, u32[]{:S(2)}) copy-start(bf16[4,12,128,32]{2,3,1,0:T(8,128)(2,1)} %copy-done.1) | copy-start | bytes 1179652
  19.1 288.9 %copy-start.4 = (bf16[4,12,128,32]{2,3,1,0:T(8,128)(2,1)S(1)}, bf16[4,12,128,32]{2,3,1,0:T(8,128)(2,1)}, u32[]{:S(2)}) copy-start(bf16[4,12,128,32]{2,3,1,0:T(8,128)(2,1)} %copy-done.3) | copy-start | bytes 1179652
  19.1 288.9 %all-to-all-start = ((bf16[128,12,128,32]{2,3,1,0:T(8,128)(2,1)}), bf16[128,12,128,32]{2,3,1,0:T(8,128)(2,1)}, u32[]{:S(2)}, u32[]{:S(2)}) async-start(bf16[128,12,128,32]{2,3,1,0:T(8,128)(2,1)} %gather_fusion), calls=%async_computation | async-start | bytes 25165824 | tf_op jit(solution)/shard_map/all_to_all | solution.py:64

commit v2 on v0

--- a/solution.py
+++ b/solution.py
@@ -4,6 +4,22 @@
 from jax.sharding import PartitionSpec as P
 
 CAP = 2
+
+
+def summed_both_ways(x, axis, dim, term):
+    size, position, span = (lax.axis_size(axis), lax.axis_index(axis), x.shape[dim])
+    right = [(i, (i + 1) % size) for i in range(size)]
+    backward = [(i, (i - 1) % size) for i in range(size)]
+    middle = size // 2
+    from_left = from_right = x
+    total = term(x, position * span)
+    for hop in range(1, middle + 1):
+        from_left = lax.ppermute(from_left, axis, right)
+        if hop < size - middle:
+            from_right = lax.ppermute(from_right, axis, backward)
+            total = total + term(from_right, (position + hop) % size * span)
+        total = total + term(from_left, (position - hop) % size * span)
+    return total
 
 
 def body(column_lists, block_values):
@@ -87,11 +103,16 @@
         "iapq,iasqc->ispc", full_rows, windows, preferred_element_type=jnp.float32
     )
     square = jnp.where(own_present[:, :, None, None], square_sum, 0.0).astype(jnp.bfloat16)
-    cube_sum = jnp.einsum(
-        "iapq,iasqc->ispc",
-        lax.all_gather(square, "cols", axis=3, tiled=True),
-        windows,
-        preferred_element_type=jnp.float32,
+    cube_sum = summed_both_ways(
+        square,
+        "cols",
+        3,
+        lambda shard, offset_2: jnp.einsum(
+            "iapq,iasqc->ispc",
+            shard,
+            lax.dynamic_slice_in_dim(windows, offset_2, shard.shape[3], axis=3),
+            preferred_element_type=jnp.float32,
+        ),
     )
     purified = jnp.where(
         own_present[:, :, None, None], 3.0 * square.astype(jnp.float32) - 2.0 * cube_sum, 0.0

time: 391 us -> 374 us (0.957)
  waiting for transfers between devices: 301 us -> 286 us
  between operations: 13.7 us -> 0.33 us
  matrix products: 7.86 us -> 16 us
    all_gather x1 -> x0, waiting for transfers between devices: 27.1 us -> none  [body(): lax.all_gather(square, 'cols', axis=3, tiled=True)]
    ppermute x0 -> x3, waiting for transfers between devices: none -> 11.6 us  [the longest x2 11.6 us: summed_both_ways(): from_left = lax.ppermute(from_left, axis, right)]
    dot_general x1 -> x4, matrix products: 5.45 us -> 14.4 us  [body(): jnp.einsum('iapq,iasqc->ispc', shard, lax.dynamic_slice_in_dim(windows, o...]
    unnamed x26 -> x18, local copies, waits for them, and re-layouts: 9.2 us -> 7.91 us
  transfers between devices with their start and end apart: 2 -> 4, of which waited for: 2 -> 3; matrix products, arithmetic and copies ran while one was open for 0% -> 3% of each run, Pallas kernels for 0% -> 0%
where the time goes in v2:
time: 374 us; the launch traced here: 373 us
  waiting for transfers between devices  286 us (76%)
  local copies, waits for them, and re-layouts  35.2 us (9%)
  other arithmetic  20.2 us (5%)
  starting transfers between devices  16 us (4%)
  matrix products  16 us (4%)
    all_to_all x1, waiting for transfers between devices, body(): lax.all_to_all(outgoing, 'rows', split_axis=0, concat_axis=0, tiled=True)  274 us
    concatenate x1, other arithmetic, body(): lookup = jnp.concatenate([arrived, local_stack], 0)  14.4 us
    dot_general x4, matrix products, body(): jnp.einsum('iapq,iasqc->ispc', shard, lax.dynamic_slice_in_dim(windows, o...  14.4 us
    all_to_all x1, starting transfers between devices, body(): lax.all_to_all(outgoing, 'rows', split_axis=0, concat_axis=0, tiled=True)  13.1 us
    ppermute x2, waiting for transfers between devices, summed_both_ways(): from_left = lax.ppermute(from_left, axis, right)  11.6 us
    gather x1, local copies, waits for them, and re-layouts, body(): picked = lookup[table_pick]  8.38 us
    gather x1, local copies, waits for them, and re-layouts, body(): outgoing = local_stack[source]  8.05 us
    unnamed x18, local copies, waits for them, and re-layouts  7.91 us
  transfers between devices with their start and end apart: 4, of which 3 were waited for; matrix products, arithmetic and copies ran while one was open for 3% of the time, Pallas kernels for 0%

profile of v2, /device:TPU:1, one launch (start us, length us, event | category | flops | bytes accessed | tf_op | source)
XLA Modules:
  0.0 373.4 jit_solution(1412319515014863604)
XLA Ops:
  1.6 2.7 select_reduce_fusion
  5.5 2.8 copy.55
  9.4 1.4 broadcast_select_fusion
  10.7 1.2 constant_dynamic-slice_fusion
  12.1 8.0 %gather_fusion = bf16[128,12,128,32]{2,3,1,0:T(8,128)(2,1)} fusion(bf16[9,12,128,32]{2,3,1,0:T(8,128)(2,1)S(1)} %pad_maximum_fusion.1, s32[1024]{0:T(1024)S(1)} %pad_clamp_fusion.1), kind=kCustom, calls=%fused_computation | custom fusion | bytes 25166336 | tf_op jit(solution)/shard_map/gather | solution.py:67
  20.1 13.1 %all-to-all-start = ((bf16[128,12,128,32]{2,3,1,0:T(8,128)(2,1)}), bf16[128,12,128,32]{2,3,1,0:T(8,128)(2,1)}, u32[]{:S(2)}, u32[]{:S(2)}) async-start(bf16[128,12,128,32]{2,3,1,0:T(8,128)(2,1)} %gather_fusion), calls=%async_computation | async-start | bytes 25165824 | tf_op jit(solution)/shard_map/all_to_all | solution.py:80
  35.0 274.0 %all-to-all-done = bf16[128,12,128,32]{2,3,1,0:T(8,128)(2,1)} async-done(((bf16[128,12,128,32]{2,3,1,0:T(8,128)(2,1)}), bf16[128,12,128,32]{2,3,1,0:T(8,128)(2,1)}, u32[]{:S(2)}, u32[]{:S(2)}) %all-to-all-start) | async-done | bytes 12582944 | tf_op jit(solution)/shard_map/all_to_all | solution.py:80
  308.9 14.4 %pad_maximum_fusion = bf16[137,12,128,32]{2,3,1,0:T(8,128)(2,1)} fusion(bf16[1,12,128,32]{2,3,1,0:T(8,128)(2,1)S(1)} %broadcast_in_dim.85, bf16[4,12,128,32]{2,3,1,0:T(8,128)(2,1)S(1)} %get-tuple-element.34, bf16[4,12,128,32]{2,3,1,0:T(8,128)(2,1)S(1)} %get-tuple-element.33, bf16[128,12,128,32]{2,3,1,0:T(8,128)(2,1)} %all-to-all-done), kind=kLoop, calls=%fused_computation.4 | loop fusion | flops 20201472 | bytes 26935296 | tf_op jit(solution)/shard_map/concatenate | solution.py:81
  323.3 8.4 %gather_fusion.2 = bf16[52,12,128,32]{2,3,1,0:T(8,128)(2,1)} fusion(bf16[137,12,128,32]{2,3,1,0:T(8,128)(2,1)} %pad_maximum_fusion, s32[1024]{0:T(1024)S(1)} %pad_clamp_fusion), kind=kCustom, calls=%fused_computation.2 | custom fusion | bytes 10223824 | tf_op jit(solution)/shard_map/gather | solution.py:82
  333.9 1.1 slice_bitcast_fusion.6
  335.0 1.1 slice_bitcast_fusion.4
  336.1 1.1 slice_bitcast_fusion.2
  337.2 1.2 slice_bitcast_fusion
  338.9 1.1 bitcast_dynamic-update-slice_fusion.6
  340.4 2.4 copy-done
  342.9 1.7 fusion.56
  344.5 1.4 collective-permute-start.1
  345.9 1.5 collective-permute-start
  347.4 5.3 %fusion.17 = f32[4,13,32,128]{3,2,1,0:T(8,128)S(1)} fusion(bf16[4,13,13,128,32]{3,4,1,2,0:T(8,128)(2,1)} %copy-done, s32[]{:T(128)S(6)} %select_n.115, bf16[4,13,32,128]{3,2,1,0:T(8,128)(2,1)S(1)} %fusion.56), kind=kOutput, calls=%fused_computation.22 | convolution fusion | flops 177209344 | bytes 6815748 | tf_op jit(solution)/shard_map/iapq,iasqc->ispc/dot_general | solution.py:110
  352.7 4.9 %collective-permute-done.1 = bf16[4,13,128,32]{2,3,1,0:T(8,128)(2,1)S(1)} collective-permute-done((bf16[4,13,128,32]{2,3,1,0:T(8,128)(2,1)S(1)}, bf16[4,13,128,32]{2,3,1,0:T(8,128)(2,1)S(1)}, u32[]{:S(2)}, u32[]{:S(2)}) %collective-permute-start.1) | collective-permute-done | bytes 426016 | tf_op jit(solution)/shard_map/ppermute | solution.py:17
  357.7 2.7 fusion.41
  360.4 2.8 fusion.38
  363.2 6.7 %collective-permute-done.2 = bf16[4,13,128,32]{2,3,1,0:T(8,128)(2,1)S(1)} collective-permute-done((bf16[4,13,128,32]{2,3,1,0:T(8,128)(2,1)S(1)}, bf16[4,13,128,32]{2,3,1,0:T(8,128)(2,1)S(1)}, u32[]{:S(2)}, u32[]{:S(2)}) %collective-permute-start.2) | collective-permute-done | bytes 426016 | tf_op jit(solution)/shard_map/ppermute | solution.py:17
  369.8 3.6 fusion.50
  (52 shorter events, 8.4 us)
Async XLA Ops:
  20.1 288.8 %all-to-all-start = ((bf16[128,12,128,32]{2,3,1,0:T(8,128)(2,1)}), bf16[128,12,128,32]{2,3,1,0:T(8,128)(2,1)}, u32[]{:S(2)}, u32[]{:S(2)}) async-start(bf16[128,12,128,32]{2,3,1,0:T(8,128)(2,1)} %gather_fusion), calls=%async_computation | async-start | bytes 25165824 | tf_op jit(solution)/shard_map/all_to_all | solution.py:80
  340.4 2.4 copy-start
  344.5 13.1 %collective-permute-start.1 = (bf16[4,13,128,32]{2,3,1,0:T(8,128)(2,1)S(1)}, bf16[4,13,128,32]{2,3,1,0:T(8,128)(2,1)S(1)}, u32[]{:S(2)}, u32[]{:S(2)}) collective-permute-start(bf16[4,13,128,32]{2,3,1,0:T(8,128)(2,1)S(1)} %bitcast.167), channel_id=1, source_target_pairs={{0,1},{1,2},{2,3},{3,0},{4,5},{5,6},{6,7},{7,4},{8,9},{9,10},{10,1... | collective-permute-start | bytes 1277960 | tf_op jit(solution)/shard_map/ppermute | solution.py:17
  345.9 11.8 %collective-permute-start = (bf16[4,13,128,32]{2,3,1,0:T(8,128)(2,1)S(1)}, bf16[4,13,128,32]{2,3,1,0:T(8,128)(2,1)S(1)}, u32[]{:S(2)}, u32[]{:S(2)}) collective-permute-start(bf16[4,13,128,32]{2,3,1,0:T(8,128)(2,1)S(1)} %bitcast.168), channel_id=1, source_target_pairs={{0,3},{1,0},{2,1},{3,2},{4,7},{5,4},{6,5},{7,6},{8,11},{9,8},{10,9... | collective-permute-start | bytes 1277960 | tf_op jit(solution)/shard_map/ppermute | solution.py:19
  347.4 10.3 %copy-start.1 = (bf16[4,13,13,128,32]{3,4,1,2,0:T(8,128)(2,1)S(1)}, bf16[4,13,13,128,32]{3,4,1,2,0:T(8,128)(2,1)}, u32[]{:S(2)}) copy-start(bf16[4,13,13,128,32]{3,4,1,2,0:T(8,128)(2,1)} %copy-done) | copy-start | bytes 16613380
  357.7 12.2 %collective-permute-start.2 = (bf16[4,13,128,32]{2,3,1,0:T(8,128)(2,1)S(1)}, bf16[4,13,128,32]{2,3,1,0:T(8,128)(2,1)S(1)}, u32[]{:S(2)}, u32[]{:S(2)}) collective-permute-start(bf16[4,13,128,32]{2,3,1,0:T(8,128)(2,1)S(1)} %collective-permute-done.1), channel_id=1, source_target_pairs={{0,1},{1,2},{2,3},{3,0},{4,5},{5,6},{6,7},{7,4},{8,9},{9,10},{10,1... | collective-permute-start | bytes 1277960 | tf_op jit(solution)/shard_map/ppermute | solution.py:17
